TPU v7x, 128 devices: a whole 4x4x4 slice. The times are simulated.
128 devices in a mesh: dp: 16 (over y, x), tensor: 8 (over z, core).
Axes of the slice: x: 4, y: 4, z: 4, core: 2. Of those that a mesh axis runs over, the one named last changes fastest.
Arguments:
- attn_out: bfloat16 [16384, 8192], P('dp', 'tensor'), may hold values from -6 to 6
- out_weight: bfloat16 [8192, 3584], P('tensor', 'dp'), may hold values from -0.0625 to 0.0625
- residual: bfloat16 [16384, 3584], P(('dp', 'tensor')), may hold values from -101 to 101
- norm_gain: float32 [3584], replicated, may hold values from 0.5 to 1.5
- expert_ids: int32 [16384, 8], P(('dp', 'tensor')), may hold values from 0 to 127, all different within a row; in each aligned block of 128 rows (0 to 127, 128 to 255, ...) at most 12 rows name the same one
- route_weight: float32 [16384, 8], P(('dp', 'tensor')), may hold values from 0.05 to 0.35
- w_gate: bfloat16 [128, 3584, 1024], P(('dp', 'tensor')), may hold values from -1 to 1
- w_up: bfloat16 [128, 3584, 1024], P(('dp', 'tensor')), may hold values from -1 to 1
- w_down: bfloat16 [128, 1024, 3584], P(('dp', 'tensor')), may hold values from -0.1875 to 0.1875
- history_x: float32 [16], replicated, may hold values from 8 to 40
- history_h: float32 [16], replicated, may hold values from 4 to 16
Outputs:
- layer_out: bfloat16 [16384, 3584], P(('dp', 'tensor'))
- new_history_x: float32 [16], replicated
- new_history_h: float32 [16], replicated
Inputs may be any that keep to these rules, and one draw needn't show every extreme that they name: `expert_ids`: among the routes of one device's 128 tokens no expert is named more than 12 times, a bound that some block reaches.
All inputs are finite; a program needn't handle non-finite values.
Results may differ from a plain program's by a relative error of at most 0.02.
Values may be sent and summed in bfloat16 or wider, within the bound.
A program may use at most 128 MiB of HBM per device.

v0:
```python
import jax
import jax.numpy as jnp
from jax import lax
from jax.sharding import PartitionSpec as P

FP8_LIMIT = 448.0


def body(
    attn_out,
    out_weight,
    residual,
    norm_gain,
    expert_ids,
    route_weight,
    w_gate,
    w_up,
    w_down,
    history_x,
    history_h,
):
    data_count = lax.axis_size("dp")
    tensor_count = lax.axis_size("tensor")
    experts = data_count * tensor_count
    local_rows = residual.shape[0]
    width = residual.shape[1]
    top_count = expert_ids.shape[1]
    capacity = max(2, 3 * local_rows * top_count // (2 * experts))
    head_terms = jnp.dot(
        attn_out,
        lax.all_gather(out_weight, "dp", axis=1, tiled=True),
        preferred_element_type=jnp.float32,
    )
    projected = lax.psum_scatter(
        head_terms.astype(jnp.bfloat16), "tensor", scatter_dimension=0, tiled=True
    ).astype(jnp.float32)
    stream = residual.astype(jnp.float32) + projected
    normed = (
        stream * lax.rsqrt(jnp.mean(stream * stream, axis=-1, keepdims=True) + 1e-06) * norm_gain
    )
    local_peak_x = jnp.max(jnp.abs(normed))
    amax_x = lax.pmax(local_peak_x, ("dp", "tensor"))
    scale_x = FP8_LIMIT / jnp.max(history_x)
    inv_x = jnp.max(history_x) / FP8_LIMIT
    scale_h = FP8_LIMIT / jnp.max(history_h)
    inv_h = jnp.max(history_h) / FP8_LIMIT
    quantized = jnp.clip(normed * scale_x, -FP8_LIMIT, FP8_LIMIT).astype(jnp.bfloat16)
    flat_ids = expert_ids.reshape(-1)
    onehot = (flat_ids[:, None] == jnp.arange(experts, dtype=jnp.int32)[None, :]).astype(jnp.int32)
    before = jnp.cumsum(onehot, axis=0) - onehot
    slot_index = jnp.sum(before * onehot, axis=-1)
    position = flat_ids * capacity + slot_index
    matches = (
        position.reshape(local_rows, top_count)[:, :, None]
        == jnp.arange(experts * capacity, dtype=jnp.int32)[None, None, :]
    )
    placing = jnp.sum(matches.astype(jnp.int32), axis=1).astype(jnp.bfloat16)
    outgoing = lax.dot_general(
        placing, quantized, (((0,), (0,)), ((), ())), preferred_element_type=jnp.float32
    )
    outgoing = outgoing.astype(jnp.bfloat16).reshape(experts, capacity, width)
    gate_matrix = w_gate[0]
    up_matrix = w_up[0]
    down_matrix = w_down[0]
    token_block = lax.all_to_all(
        outgoing, ("dp", "tensor"), split_axis=0, concat_axis=0, tiled=True
    )
    source_count = token_block.shape[0]
    slot_count = token_block.shape[1]
    flat_rows = token_block.reshape(source_count * slot_count, width)
    gate = jnp.dot(flat_rows, gate_matrix, preferred_element_type=jnp.float32) * inv_x
    upper = jnp.dot(flat_rows, up_matrix, preferred_element_type=jnp.float32) * inv_x
    hidden = jax.nn.silu(gate) * upper
    row_peaks = jnp.max(jnp.abs(hidden), axis=1).reshape(source_count, slot_count)
    hidden_q = jnp.clip(hidden * scale_h, -FP8_LIMIT, FP8_LIMIT).astype(jnp.bfloat16)
    expert_out = (
        jnp.dot(hidden_q, down_matrix, preferred_element_type=jnp.float32) * inv_h
    ).astype(jnp.bfloat16)
    expert_out, row_peaks = (expert_out.reshape(source_count, slot_count, width), row_peaks)
    returned = lax.all_to_all(expert_out, ("dp", "tensor"), split_axis=0, concat_axis=0, tiled=True)
    returned_flat = returned.reshape(experts * capacity, width)
    picked = returned_flat[position].reshape(local_rows, top_count, width)
    mixture = jnp.sum(picked.astype(jnp.float32) * route_weight[:, :, None], axis=1)
    layer_out = (stream + mixture).astype(jnp.bfloat16)
    local_peak_h = jnp.max(row_peaks)
    amax_h = lax.pmax(local_peak_h, ("dp", "tensor"))
    new_history_x = jnp.concatenate([amax_x[None], history_x[:-1]])
    new_history_h = jnp.concatenate([amax_h[None], history_h[:-1]])
    return (layer_out, new_history_x, new_history_h)


def solution(mesh):
    in_specs = (
        P("dp", "tensor"),
        P("tensor", "dp"),
        P(("dp", "tensor"), None),
        P(),
        P(("dp", "tensor"), None),
        P(("dp", "tensor"), None),
        P(("dp", "tensor"), None, None),
        P(("dp", "tensor"), None, None),
        P(("dp", "tensor"), None, None),
        P(),
        P(),
    )
    out_specs = (P(("dp", "tensor"), None), P(), P())
    return jax.shard_map(body, mesh=mesh, in_specs=in_specs, out_specs=out_specs, check_vma=False)
```

profile of v0, /device:TPU:1, one launch (start us, length us, event | category | flops | bytes accessed | tf_op | source)
XLA Modules:
  0.0 784.3 jit_solution(17509006008396059354)
XLA Ops:
  7.2 0.7 all-gather.2.cloned.1.call-update
  8.0 71.4 %all-gather.2.cloned.1.call-done = bf16[1024,3584]{0,1:T(8,128)(2,1)} async-done(((bf16[1024,224]{0,1:T(8,128)(2,1)}), bf16[1024,3584]{0,1:T(8,128)(2,1)}) %all-gather.2.cloned.1.call-update) | async-done | bytes 7340048 | tf_op jit(solution)/shard_map/all_gather | solution.py:31
  79.4 12.8 %convolution_convert_fusion.1 = bf16[1024,3584]{1,0:T(8,128)(2,1)} fusion(bf16[1024,1024]{1,0:T(8,128)(2,1)S(1)} %copy-done, bf16[1024,3584]{0,1:T(8,128)(2,1)} %all-gather.2.cloned.1.call-done), kind=kOutput, calls=%fused_computation.5 | convolution fusion | flops 7519862784 | bytes 16777216 | tf_op jit(solution)/shard_map/dot_general | solution.py:29
  92.3 0.6 copy-done.6
  92.9 0.1 copy.22
  93.2 0.1 copy.25
  93.3 0.2 fusion.18
  93.6 0.1 copy.26
  93.7 0.4 fusion.17
  94.2 0.6 reduce_max.35
  95.5 2.5 convert_reduce_fusion
  98.0 41.1 %reduce-scatter.2.cloned.1.call-done = bf16[128,3584]{1,0:T(8,128)(2,1)} async-done(((bf16[1024,3584]{1,0:T(8,128)(2,1)}), bf16[128,3584]{1,0:T(8,128)(2,1)}) %reduce-scatter.2.cloned.1.call-update) | async-done | bytes 917520 | tf_op jit(solution)/shard_map/reduce_scatter | solution.py:34
  139.1 1.6 multiply_reduce_fusion
  140.7 7.1 convolution_convert_fusion
  147.8 17.1 %reshape.85 = bf16[128,12,3584]{2,1,0:T(8,128)(2,1)} reshape(bf16[1536,3584]{1,0:T(8,128)(2,1)} %convolution_convert_fusion) | data formatting | bytes 22020096 | tf_op jit(solution)/shard_map/reshape | solution.py:61
  164.9 8.8 %all-to-all-start = ((bf16[128,12,3584]{2,1,0:T(8,128)(2,1)}), bf16[128,12,3584]{2,1,0:T(8,128)(2,1)}, u32[]{:S(2)}, u32[]{:S(2)}) async-start(bf16[128,12,3584]{2,1,0:T(8,128)(2,1)} %reshape.85), calls=%async_computation.1 | async-start | bytes 29360128 | tf_op jit(solution)/shard_map/all_to_all | solution.py:65
  174.3 0.6 reduce_max.36
  176.3 190.6 %all-to-all-done = bf16[128,12,3584]{2,1,0:T(8,128)(2,1)} async-done(((bf16[128,12,3584]{2,1,0:T(8,128)(2,1)}), bf16[128,12,3584]{2,1,0:T(8,128)(2,1)}, u32[]{:S(2)}, u32[]{:S(2)}) %all-to-all-start) | async-done | bytes 11010080 | tf_op jit(solution)/shard_map/all_to_all | solution.py:65
  366.9 17.1 %reshape.86 = bf16[1536,3584]{1,0:T(8,128)(2,1)} reshape(bf16[128,12,3584]{2,1,0:T(8,128)(2,1)} %all-to-all-done) | data formatting | bytes 22020096 | tf_op jit(solution)/shard_map/reshape | solution.py:70
  384.0 16.5 %fusion.2 = f32[1536,1024]{1,0:T(8,128)S(1)} fusion(bf16[1536,3584]{1,0:T(8,128)(2,1)} %reshape.86, bf16[1,3584,1024]{2,1,0:T(8,128)(2,1)} %param.18), kind=kOutput, calls=%fused_computation.7 | convolution fusion | flops 11274289152 | bytes 24641536 | tf_op jit(solution)/shard_map/dot_general | solution.py:72
  400.6 18.3 %abs_reduce_fusion = (f32[]{:T(128)}, f32[1536,1024]{1,0:T(8,128)}) fusion(f32[1536,1024]{1,0:T(8,128)S(1)} %fusion.2, f32[]{:T(128)S(6)} %div.25, bf16[1536,3584]{1,0:T(8,128)(2,1)S(1)} %copy-done.2, bf16[1,3584,1024]{2,1,0:T(8,128)(2,1)} %param.17), kind=kOutput, calls=%fused_computation.11 | convolution fusion | flops 11288444928 | bytes 30933000 | tf_op jit(solution)/shard_map/dot_general | solution.py:71
  418.8 17.2 %multiply_convert_fusion = bf16[1536,3584]{1,0:T(8,128)(2,1)} fusion(f32[]{:T(128)S(6)} %div.28, bf16[1,1024,3584]{2,1,0:T(8,128)(2,1)S(1)} %bitcast.41, f32[1536,1024]{1,0:T(8,128)} %get-tuple-element.10, f32[]{:T(128)S(6)} %div.27), kind=kOutput, calls=%fused_computation.1 | convolution fusion | flops 11290017792 | bytes 24641544 | tf_op jit(solution)/shard_map/dot_general | solution.py:77
  436.0 17.1 %reshape.87 = bf16[128,12,3584]{2,1,0:T(8,128)(2,1)} reshape(bf16[1536,3584]{1,0:T(8,128)(2,1)} %multiply_convert_fusion) | data formatting | bytes 22020096 | tf_op jit(solution)/shard_map/reshape | solution.py:79
  453.1 11.7 %all-to-all-start.1 = ((bf16[128,12,3584]{2,1,0:T(8,128)(2,1)}), bf16[128,12,3584]{2,1,0:T(8,128)(2,1)}, u32[]{:S(2)}, u32[]{:S(2)}) async-start(bf16[128,12,3584]{2,1,0:T(8,128)(2,1)} %reshape.87), calls=%async_computation.2 | async-start | bytes 29360128 | tf_op jit(solution)/shard_map/all_to_all | solution.py:80
  464.9 0.1 copy.27
  465.0 191.2 %all-to-all-done.1 = bf16[128,12,3584]{2,1,0:T(8,128)(2,1)} async-done(((bf16[128,12,3584]{2,1,0:T(8,128)(2,1)}), bf16[128,12,3584]{2,1,0:T(8,128)(2,1)}, u32[]{:S(2)}, u32[]{:S(2)}) %all-to-all-start.1) | async-done | bytes 11010080 | tf_op jit(solution)/shard_map/all_to_all | solution.py:80
  656.2 17.1 %reshape.88 = bf16[1536,3584]{1,0:T(8,128)(2,1)} reshape(bf16[128,12,3584]{2,1,0:T(8,128)(2,1)} %all-to-all-done.1) | data formatting | bytes 22020096 | tf_op jit(solution)/shard_map/reshape | solution.py:81
  673.3 19.5 %gather_fusion = bf16[1024,3584]{1,0:T(8,128)(2,1)} fusion(bf16[1536,3584]{1,0:T(8,128)(2,1)} %reshape.88, s32[1024]{0:T(1024)S(1)} %broadcast_clamp_fusion), kind=kCustom, calls=%fused_computation | custom fusion | bytes 14684160 | tf_op jit(solution)/shard_map/gather | solution.py:82
  692.8 9.9 %fusion = f32[128,3584]{1,0:T(8,128)S(1)} fusion(bf16[1024,3584]{1,0:T(8,128)(2,1)} %gather_fusion, f32[128,8]{1,0:T(8,128)S(1)} %copy.27), kind=kLoop, calls=%fused_computation.4 | loop fusion | flops 10551296 | bytes 9179136 | tf_op jit(solution)/shard_map/reduce_sum | solution.py:83
  702.7 2.0 abs_reduce_fusion.1
  704.7 70.9 %all-reduce = (f32[1]{0:T(128)}, f32[1]{0:T(128)}) all-reduce(f32[1]{0:T(128)} %bitcast.9, f32[1]{0:T(128)} %bitcast.10), channel_id=1, replica_groups=mesh['dp'=16,'tensor'=8] {'dp','tensor'}, use_global_device_ids=true, to_apply=%region_10.11 | all-reduce | flops 2 | bytes 16 | tf_op jit(solution)/shard_map/pmax | solution.py:42
  775.6 1.8 pad_maximum_fusion
  (39 shorter events, 0.6 us)
Async XLA Ops:
  7.2 72.2 %copy-start = (bf16[1024,1024]{1,0:T(8,128)(2,1)S(1)}, bf16[1024,1024]{1,0:T(8,128)(2,1)}, u32[]{:S(2)}) copy-start(bf16[1024,1024]{1,0:T(8,128)(2,1)} %param.11) | copy-start | bytes 6291460
  7.2 72.2 %all-gather.2.cloned.1.call-start = ((), (), s32[]{:S(2)}) async-start(), calls=%async_computation.3 | async-start | bytes 7798784 | tf_op jit(solution)/shard_map/all_gather | solution.py:31
  7.9 131.2 %reduce-scatter.2.cloned.1.call-start = ((), (), s32[]{:S(2)}) async-start(), calls=%async_computation.4 | async-start | bytes 8257536 | tf_op jit(solution)/shard_map/reduce_scatter | solution.py:34
  92.2 0.7 copy-start.6
  92.2 1.9 copy-start.9
  92.2 46.9 %copy-start.3 = (bf16[128,3584]{1,0:T(8,128)(2,1)S(1)}, bf16[128,3584]{1,0:T(8,128)(2,1)}, u32[]{:S(2)}) copy-start(bf16[128,3584]{1,0:T(8,128)(2,1)} %param.13) | copy-start | bytes 2752516
  92.2 48.4 %copy-start.5 = (f32[3584]{0:T(1024)S(1)}, f32[3584]{0:T(1024)}, u32[]{:S(2)}) copy-start(f32[3584]{0:T(1024)} %param.14) | copy-start | bytes 43012
  164.9 9.5 %copy-start.8 = (f32[16]{0:T(128)S(1)}, f32[16]{0:T(128)}, u32[]{:S(2)}) copy-start(f32[16]{0:T(128)} %param.21) | copy-start | bytes 196
  164.9 202.0 %all-to-all-start = ((bf16[128,12,3584]{2,1,0:T(8,128)(2,1)}), bf16[128,12,3584]{2,1,0:T(8,128)(2,1)}, u32[]{:S(2)}, u32[]{:S(2)}) async-start(bf16[128,12,3584]{2,1,0:T(8,128)(2,1)} %reshape.85), calls=%async_computation.1 | async-start | bytes 29360128 | tf_op jit(solution)/shard_map/all_to_all | solution.py:65
  384.0 16.6 %copy-start.2 = (bf16[1536,3584]{1,0:T(8,128)(2,1)S(1)}, bf16[1536,3584]{1,0:T(8,128)(2,1)}, u32[]{:S(2)}) copy-start(bf16[1536,3584]{1,0:T(8,128)(2,1)} %reshape.86) | copy-start | bytes 33030148
  384.0 34.8 %slice-start = ((s8[7340032]{0:T(1024)(128)(4,1)}), s8[4194304]{0:T(1024)(128)(4,1)S(1)}, s32[]{:S(2)}) async-start(s8[7340032]{0:T(1024)(128)(4,1)} %bitcast.40), calls=%async_computation.5 | async-start | bytes 8388608
  400.6 18.3 %slice-start.1 = ((s8[7340032]{0:T(1024)(128)(4,1)}), s8[3145728]{0:T(1024)(128)(4,1)S(1)}, s32[]{:S(2)}) async-start(s8[7340032]{0:T(1024)(128)(4,1)} %bitcast.40), calls=%async_computation.6 | async-start | bytes 6291456
  453.1 11.8 %copy-start.7 = (f32[128,8]{0,1:T(8,128)S(1)}, f32[128,8]{0,1:T(8,128)}, u32[]{:S(2)}) copy-start(f32[128,8]{0,1:T(8,128)} %param.16) | copy-start | bytes 12292
  453.1 203.1 %all-to-all-start.1 = ((bf16[128,12,3584]{2,1,0:T(8,128)(2,1)}), bf16[128,12,3584]{2,1,0:T(8,128)(2,1)}, u32[]{:S(2)}, u32[]{:S(2)}) async-start(bf16[128,12,3584]{2,1,0:T(8,128)(2,1)} %reshape.87), calls=%async_computation.2 | async-start | bytes 29360128 | tf_op jit(solution)/shard_map/all_to_all | solution.py:80
  673.3 104.1 %copy-start.1 = (bf16[1024,1024]{1,0:T(8,128)(2,1)S(1)}, bf16[1024,1024]{1,0:T(8,128)(2,1)}, u32[]{:S(2)}) copy-start(bf16[1024,1024]{1,0:T(8,128)(2,1)} %param.11) | copy-start | bytes 6291460
  692.8 9.9 %copy-start.4 = (bf16[128,3584]{1,0:T(8,128)(2,1)S(1)}, bf16[128,3584]{1,0:T(8,128)(2,1)}, u32[]{:S(2)}) copy-start(bf16[128,3584]{1,0:T(8,128)(2,1)} %reduce-scatter.2.cloned.1.call-done) | copy-start | bytes 2752516
Sparse Core Ops, SparseCore 0:
  10.2 69.2 all-gather.1
  92.4 46.6 reduce-scatter.1
where the time goes:
time: 786 us; the launch traced here: 784 us
  waiting for transfers between devices  495 us (63%)
  local copies, waits for them, and re-layouts  89.4 us (11%)
  matrix products  71.9 us (9%)
  blocking collectives  70.9 us (9%)
  starting transfers between devices  20.6 us (3%)
  other arithmetic  19.6 us (2%)
  between operations  16.9 us (2%)
    all_to_all x1, waiting for transfers between devices, body(): lax.all_to_all(expert_out, ('dp', 'tensor'), split_axis=0, concat_axis=0,...  191 us
    all_to_all x1, waiting for transfers between devices, body(): lax.all_to_all(outgoing, ('dp', 'tensor'), split_axis=0, concat_axis=0, t...  191 us
    all_gather x1, waiting for transfers between devices, body(): lax.all_gather(out_weight, 'dp', axis=1, tiled=True)  71.4 us
    pmax x1, blocking collectives, body(): amax_x = lax.pmax(local_peak_x, ('dp', 'tensor'))  70.9 us
    reduce_scatter x1, waiting for transfers between devices, body(): lax.psum_scatter(head_terms.astype(jnp.bfloat16), 'tensor', scatter_dimen...  41.1 us
    gather x1, local copies, waits for them, and re-layouts, body(): picked = returned_flat[position].reshape(local_rows, top_count, width)  19.5 us
    dot_general x1, matrix products, body(): jnp.dot(flat_rows, gate_matrix, preferred_element_type=jnp.float32) * inv_x  18.3 us
    dot_general x1, matrix products, body(): jnp.dot(hidden_q, down_matrix, preferred_element_type=jnp.float32) * inv_h  17.2 us
  transfers between devices with their start and end apart: 4, of which 4 were waited for; matrix products, arithmetic and copies ran while one was open for 1% of the time, Pallas kernels for 0%

commit v1 on v0

--- a/solution.py
+++ b/solution.py
@@ -4,6 +4,24 @@
 from jax.sharding import PartitionSpec as P
 
 FP8_LIMIT = 448.0
+
+
+def collect(shard, axis, dim):
+    ways, here, hop = (lax.axis_size(axis), lax.axis_index(axis), shard.shape[dim])
+    shape = [n * ways if d == dim else n for d, n in enumerate(shard.shape)]
+    full = lax.dynamic_update_slice_in_dim(
+        jnp.zeros(shape, shard.dtype), shard, here * hop, axis=dim
+    )
+    going_up = going_down = shard
+    for far in range(1, ways // 2 + 1):
+        going_up = lax.ppermute(going_up, axis, [(d, (d + 1) % ways) for d in range(ways)])
+        full = lax.dynamic_update_slice_in_dim(full, going_up, (here - far) % ways * hop, axis=dim)
+        if 2 * far < ways:
+            going_down = lax.ppermute(going_down, axis, [(d, (d - 1) % ways) for d in range(ways)])
+            full = lax.dynamic_update_slice_in_dim(
+                full, going_down, (here + far) % ways * hop, axis=dim
+            )
+    return full
 
 
 def body(
@@ -26,11 +44,7 @@
     width = residual.shape[1]
     top_count = expert_ids.shape[1]
     capacity = max(2, 3 * local_rows * top_count // (2 * experts))
-    head_terms = jnp.dot(
-        attn_out,
-        lax.all_gather(out_weight, "dp", axis=1, tiled=True),
-        preferred_element_type=jnp.float32,
-    )
+    head_terms = jnp.dot(attn_out, collect(out_weight, "dp", 1), preferred_element_type=jnp.float32)
     projected = lax.psum_scatter(
         head_terms.astype(jnp.bfloat16), "tensor", scatter_dimension=0, tiled=True
     ).astype(jnp.float32)

time: 786 us -> 832 us (1.059)
  starting transfers between devices: 20.6 us -> 59.2 us
  local copies, waits for them, and re-layouts: 89.4 us -> 104 us
  waiting for transfers between devices: 495 us -> 485 us
    all_gather x1 -> x0, waiting for transfers between devices: 71.4 us -> none  [body(): lax.all_gather(out_weight, 'dp', axis=1, tiled=True)]
    ppermute x0 -> x15, waiting for transfers between devices: none -> 59.3 us  [the longest x8 58 us: collect(): lax.ppermute(going_up, axis, [(d, (d + 1) % ways) for d in range(ways)])]
    ppermute x0 -> x15, starting transfers between devices: none -> 35.5 us  [the longest x7 33 us: collect(): lax.ppermute(going_down, axis, [(d, (d - 1) % ways) for d in range(ways)])]
    unnamed x26 -> x45, local copies, waits for them, and re-layouts: 0.9 us -> 11 us
  transfers between devices with their start and end apart: 4 -> 18, of which waited for: 4 -> 13; matrix products, arithmetic and copies ran while one was open for 1% -> 1% of each run, Pallas kernels for 0% -> 0%
where the time goes in v1:
time: 832 us; the launch traced here: 824 us
  waiting for transfers between devices  485 us (58%)
  local copies, waits for them, and re-layouts  104 us (12%)
  blocking collectives  69.5 us (8%)
  matrix products  68.9 us (8%)
  starting transfers between devices  59.2 us (7%)
  other arithmetic  19.6 us (2%)
  between operations  17.7 us (2%)
    all_to_all x1, waiting for transfers between devices, body(): lax.all_to_all(expert_out, ('dp', 'tensor'), split_axis=0, concat_axis=0,...  191 us
    all_to_all x1, waiting for transfers between devices, body(): lax.all_to_all(outgoing, ('dp', 'tensor'), split_axis=0, concat_axis=0, t...  189 us
    pmax x1, blocking collectives, body(): amax_x = lax.pmax(local_peak_x, ('dp', 'tensor'))  69.5 us
    ppermute x8, waiting for transfers between devices, collect(): lax.ppermute(going_up, axis, [(d, (d + 1) % ways) for d in range(ways)])  58 us
    reduce_scatter x1, waiting for transfers between devices, body(): lax.psum_scatter(head_terms.astype(jnp.bfloat16), 'tensor', scatter_dimen...  46.1 us
    ppermute x7, starting transfers between devices, collect(): lax.ppermute(going_down, axis, [(d, (d - 1) % ways) for d in range(ways)])  33 us
    gather x1, local copies, waits for them, and re-layouts, body(): picked = returned_flat[position].reshape(local_rows, top_count, width)  19.5 us
    dot_general x1, matrix products, body(): jnp.dot(flat_rows, gate_matrix, preferred_element_type=jnp.float32) * inv_x  18.3 us
  transfers between devices with their start and end apart: 18, of which 13 were waited for; matrix products, arithmetic and copies ran while one was open for 1% of the time, Pallas kernels for 0%

profile of v1, /device:TPU:1, one launch (start us, length us, event | category | flops | bytes accessed | tf_op | source)
XLA Modules:
  0.0 824.3 jit_solution(4118762765193191161)
XLA Ops:
  9.3 3.8 collective-permute-start.1
  13.1 10.3 %collective-permute-done = bf16[1024,224]{0,1:T(8,128)(2,1)S(1)} collective-permute-done((bf16[1024,224]{0,1:T(8,128)(2,1)}, bf16[1024,224]{0,1:T(8,128)(2,1)S(1)}, u32[]{:S(2)}, u32[]{:S(2)}) %collective-permute-start) | collective-permute-done | bytes 458784 | tf_op jit(solution)/shard_map/ppermute | solution.py:17
  23.5 4.8 collective-permute-start.3
  28.3 9.3 %collective-permute-done.2 = bf16[1024,224]{0,1:T(8,128)(2,1)S(1)} collective-permute-done((bf16[1024,224]{0,1:T(8,128)(2,1)S(1)}, bf16[1024,224]{0,1:T(8,128)(2,1)S(1)}, u32[]{:S(2)}, u32[]{:S(2)}) %collective-permute-start.2) | collective-permute-done | bytes 458784 | tf_op jit(solution)/shard_map/ppermute | solution.py:17
  37.5 4.8 collective-permute-start.5
  42.3 8.3 %collective-permute-done.4 = bf16[1024,224]{0,1:T(8,128)(2,1)S(1)} collective-permute-done((bf16[1024,224]{0,1:T(8,128)(2,1)S(1)}, bf16[1024,224]{0,1:T(8,128)(2,1)S(1)}, u32[]{:S(2)}, u32[]{:S(2)}) %collective-permute-start.4) | collective-permute-done | bytes 458784 | tf_op jit(solution)/shard_map/ppermute | solution.py:17
  50.7 4.8 collective-permute-start.7
  55.4 7.4 collective-permute-done.6
  64.3 4.5 collective-permute-start.9
  68.9 5.4 collective-permute-done.8
  74.5 5.5 collective-permute-start.11
  81.1 4.0 collective-permute-done.10
  87.3 4.9 collective-permute-start.13
  97.6 9.6 %collective-permute-done.14 = bf16[1024,224]{0,1:T(8,128)(2,1)S(1)} collective-permute-done((bf16[1024,224]{0,1:T(8,128)(2,1)S(1)}, bf16[1024,224]{0,1:T(8,128)(2,1)S(1)}, u32[]{:S(2)}, u32[]{:S(2)}) %collective-permute-start.14) | collective-permute-done | bytes 458784 | tf_op jit(solution)/shard_map/ppermute | solution.py:17
  107.3 9.7 %fusion.6 = bf16[1024,3584]{0,1:T(8,128)(2,1)} fusion(bf16[1024,3584]{0,1:T(8,128)(2,1)S(1)} %constant_dynamic-update-slice_fusion, bf16[1024,1024]{1,0:T(8,128)(2,1)S(1)} %copy-done), kind=kOutput, calls=%fused_computation.11 | convolution fusion | flops 7519862784 | bytes 16777216 | tf_op jit(solution)/shard_map/dot_general | solution.py:47
  117.0 10.1 %copy.40 = bf16[1024,3584]{1,0:T(8,128)(2,1)} copy(bf16[1024,3584]{0,1:T(8,128)(2,1)} %fusion.6) | data formatting | bytes 14680064
  132.9 46.1 %reduce-scatter.4.cloned.1.call-done = bf16[128,3584]{1,0:T(8,128)(2,1)} async-done(((bf16[1024,3584]{1,0:T(8,128)(2,1)}), bf16[128,3584]{1,0:T(8,128)(2,1)}) %reduce-scatter.4.cloned.1.call-update) | async-done | bytes 917520 | tf_op jit(solution)/shard_map/reduce_scatter | solution.py:48
  180.5 7.1 convolution_convert_fusion
  187.7 17.0 %reshape.85 = bf16[128,12,3584]{2,1,0:T(8,128)(2,1)} reshape(bf16[1536,3584]{1,0:T(8,128)(2,1)} %convolution_convert_fusion) | data formatting | bytes 22020096 | tf_op jit(solution)/shard_map/reshape | solution.py:75
  204.7 9.2 %all-to-all-start = ((bf16[128,12,3584]{2,1,0:T(8,128)(2,1)}), bf16[128,12,3584]{2,1,0:T(8,128)(2,1)}, u32[]{:S(2)}, u32[]{:S(2)}) async-start(bf16[128,12,3584]{2,1,0:T(8,128)(2,1)} %reshape.85), calls=%async_computation | async-start | bytes 29360128 | tf_op jit(solution)/shard_map/all_to_all | solution.py:79
  216.5 188.8 %all-to-all-done = bf16[128,12,3584]{2,1,0:T(8,128)(2,1)} async-done(((bf16[128,12,3584]{2,1,0:T(8,128)(2,1)}), bf16[128,12,3584]{2,1,0:T(8,128)(2,1)}, u32[]{:S(2)}, u32[]{:S(2)}) %all-to-all-start) | async-done | bytes 11010080 | tf_op jit(solution)/shard_map/all_to_all | solution.py:79
  405.3 17.1 %reshape.86 = bf16[1536,3584]{1,0:T(8,128)(2,1)} reshape(bf16[128,12,3584]{2,1,0:T(8,128)(2,1)} %all-to-all-done) | data formatting | bytes 22020096 | tf_op jit(solution)/shard_map/reshape | solution.py:84
  422.4 16.5 %fusion.2 = f32[1536,1024]{1,0:T(8,128)S(1)} fusion(bf16[1536,3584]{1,0:T(8,128)(2,1)} %reshape.86, bf16[1,3584,1024]{2,1,0:T(8,128)(2,1)} %param.18), kind=kOutput, calls=%fused_computation.7 | convolution fusion | flops 11274289152 | bytes 24641536 | tf_op jit(solution)/shard_map/dot_general | solution.py:86
  439.0 18.3 %abs_reduce_fusion = (f32[]{:T(128)}, f32[1536,1024]{1,0:T(8,128)}) fusion(f32[1536,1024]{1,0:T(8,128)S(1)} %fusion.2, f32[]{:T(128)S(6)} %div.25, bf16[1536,3584]{1,0:T(8,128)(2,1)S(1)} %copy-done.2, bf16[1,3584,1024]{2,1,0:T(8,128)(2,1)} %param.17), kind=kOutput, calls=%fused_computation.12 | convolution fusion | flops 11288444928 | bytes 30933000 | tf_op jit(solution)/shard_map/dot_general | solution.py:85
  457.3 17.2 %multiply_convert_fusion = bf16[1536,3584]{1,0:T(8,128)(2,1)} fusion(f32[]{:T(128)S(6)} %div.28, bf16[1,1024,3584]{2,1,0:T(8,128)(2,1)S(1)} %bitcast.44, f32[1536,1024]{1,0:T(8,128)} %get-tuple-element.16, f32[]{:T(128)S(6)} %div.27), kind=kOutput, calls=%fused_computation.1 | convolution fusion | flops 11290017792 | bytes 24641544 | tf_op jit(solution)/shard_map/dot_general | solution.py:91
  474.5 17.0 %reshape.87 = bf16[128,12,3584]{2,1,0:T(8,128)(2,1)} reshape(bf16[1536,3584]{1,0:T(8,128)(2,1)} %multiply_convert_fusion) | data formatting | bytes 22020096 | tf_op jit(solution)/shard_map/reshape | solution.py:93
  491.6 14.4 %all-to-all-start.1 = ((bf16[128,12,3584]{2,1,0:T(8,128)(2,1)}), bf16[128,12,3584]{2,1,0:T(8,128)(2,1)}, u32[]{:S(2)}, u32[]{:S(2)}) async-start(bf16[128,12,3584]{2,1,0:T(8,128)(2,1)} %reshape.87), calls=%async_computation.1 | async-start | bytes 29360128 | tf_op jit(solution)/shard_map/all_to_all | solution.py:94
  506.2 191.2 %all-to-all-done.1 = bf16[128,12,3584]{2,1,0:T(8,128)(2,1)} async-done(((bf16[128,12,3584]{2,1,0:T(8,128)(2,1)}), bf16[128,12,3584]{2,1,0:T(8,128)(2,1)}, u32[]{:S(2)}, u32[]{:S(2)}) %all-to-all-start.1) | async-done | bytes 11010080 | tf_op jit(solution)/shard_map/all_to_all | solution.py:94
  697.4 17.1 %reshape.88 = bf16[1536,3584]{1,0:T(8,128)(2,1)} reshape(bf16[128,12,3584]{2,1,0:T(8,128)(2,1)} %all-to-all-done.1) | data formatting | bytes 22020096 | tf_op jit(solution)/shard_map/reshape | solution.py:95
  714.5 19.5 %gather_fusion = bf16[1024,3584]{1,0:T(8,128)(2,1)} fusion(bf16[1536,3584]{1,0:T(8,128)(2,1)} %reshape.88, s32[1024]{0:T(1024)S(1)} %broadcast_clamp_fusion), kind=kCustom, calls=%fused_computation | custom fusion | bytes 14684160 | tf_op jit(solution)/shard_map/gather | solution.py:96
  734.0 9.9 %fusion = f32[128,3584]{1,0:T(8,128)S(1)} fusion(bf16[1024,3584]{1,0:T(8,128)(2,1)} %gather_fusion, f32[128,8]{1,0:T(8,128)S(1)} %copy.39), kind=kLoop, calls=%fused_computation.4 | loop fusion | flops 10551296 | bytes 9179136 | tf_op jit(solution)/shard_map/reduce_sum | solution.py:97
  745.9 69.5 %all-reduce = (f32[1]{0:T(128)}, f32[1]{0:T(128)}) all-reduce(f32[1]{0:T(128)} %bitcast.10, f32[1]{0:T(128)} %bitcast.11), channel_id=1, replica_groups=mesh['dp'=16,'tensor'=8] {'dp','tensor'}, use_global_device_ids=true, to_apply=%region_10.11 | all-reduce | flops 2 | bytes 16 | tf_op jit(solution)/shard_map/pmax | solution.py:56
  (102 shorter events, 23.4 us)
Async XLA Ops:
  7.2 100.1 %copy-start = (bf16[1024,1024]{1,0:T(8,128)(2,1)S(1)}, bf16[1024,1024]{1,0:T(8,128)(2,1)}, u32[]{:S(2)}) copy-start(bf16[1024,1024]{1,0:T(8,128)(2,1)} %param.11) | copy-start | bytes 6291460
  7.2 57.0 %copy-start.5 = (bf16[1024,224]{0,1:T(8,128)(2,1)S(1)}, bf16[1024,224]{0,1:T(8,128)(2,1)}, u32[]{:S(2)}) copy-start(bf16[1024,224]{0,1:T(8,128)(2,1)} %param.12) | copy-start | bytes 1376260
  7.2 171.8 %reduce-scatter.4.cloned.1.call-start = ((), (), s32[]{:S(2)}) async-start(), calls=%async_computation.3 | async-start | bytes 8257536 | tf_op jit(solution)/shard_map/reduce_scatter | solution.py:48
  7.2 16.2 %collective-permute-start = (bf16[1024,224]{0,1:T(8,128)(2,1)}, bf16[1024,224]{0,1:T(8,128)(2,1)S(1)}, u32[]{:S(2)}, u32[]{:S(2)}) collective-permute-start(bf16[1024,224]{0,1:T(8,128)(2,1)} %param.12), channel_id=1, source_target_pairs={{0,8},{8,16},{16,24},{24,32},{32,40},{40,48},{48,56},{56,64},{64,7... | collective-permute-start | bytes 1376264 | tf_op jit(solution)/shard_map/ppermute | solution.py:17
  9.3 14.1 %collective-permute-start.1 = (bf16[1024,224]{0,1:T(8,128)(2,1)}, bf16[1024,224]{0,1:T(8,128)(2,1)S(1)}, u32[]{:S(2)}, u32[]{:S(2)}) collective-permute-start(bf16[1024,224]{0,1:T(8,128)(2,1)} %param.12), channel_id=1, source_target_pairs={{0,120},{8,0},{16,8},{24,16},{32,24},{40,32},{48,40},{56,48},{64,5... | collective-permute-start | bytes 1376264 | tf_op jit(solution)/shard_map/ppermute | solution.py:20
  23.5 14.0 %collective-permute-start.2 = (bf16[1024,224]{0,1:T(8,128)(2,1)S(1)}, bf16[1024,224]{0,1:T(8,128)(2,1)S(1)}, u32[]{:S(2)}, u32[]{:S(2)}) collective-permute-start(bf16[1024,224]{0,1:T(8,128)(2,1)S(1)} %collective-permute-done), channel_id=1, source_target_pairs={{0,8},{8,16},{16,24},{24,32},{32,40},{40,48},{48,56},{56,64},{64,7... | collective-permute-start | bytes 1376264 | tf_op jit(solution)/shard_map/ppermute | solution.py:17
  23.5 18.8 %copy-start.8 = (bf16[1024,224]{0,1:T(8,128)(2,1)}, bf16[1024,224]{0,1:T(8,128)(2,1)S(1)}, u32[]{:S(2)}) copy-start(bf16[1024,224]{0,1:T(8,128)(2,1)S(1)} %collective-permute-done.1) | copy-start | bytes 1376260
  23.5 14.0 %collective-permute-start.3 = (bf16[1024,224]{0,1:T(8,128)(2,1)S(1)}, bf16[1024,224]{0,1:T(8,128)(2,1)S(1)}, u32[]{:S(2)}, u32[]{:S(2)}) collective-permute-start(bf16[1024,224]{0,1:T(8,128)(2,1)S(1)} %collective-permute-done.1), channel_id=1, source_target_pairs={{0,120},{8,0},{16,8},{24,16},{32,24},{40,32},{48,40},{56,48},{64,5... | collective-permute-start | bytes 1376264 | tf_op jit(solution)/shard_map/ppermute | solution.py:20
  37.5 13.1 %collective-permute-start.4 = (bf16[1024,224]{0,1:T(8,128)(2,1)S(1)}, bf16[1024,224]{0,1:T(8,128)(2,1)S(1)}, u32[]{:S(2)}, u32[]{:S(2)}) collective-permute-start(bf16[1024,224]{0,1:T(8,128)(2,1)S(1)} %collective-permute-done.2), channel_id=1, source_target_pairs={{0,8},{8,16},{16,24},{24,32},{32,40},{40,48},{48,56},{56,64},{64,7... | collective-permute-start | bytes 1376264 | tf_op jit(solution)/shard_map/ppermute | solution.py:17
  37.5 25.3 %copy-start.6 = (bf16[1024,224]{0,1:T(8,128)(2,1)}, bf16[1024,224]{0,1:T(8,128)(2,1)S(1)}, u32[]{:S(2)}) copy-start(bf16[1024,224]{0,1:T(8,128)(2,1)S(1)} %collective-permute-done.3) | copy-start | bytes 1376260
  37.5 13.1 %collective-permute-start.5 = (bf16[1024,224]{0,1:T(8,128)(2,1)S(1)}, bf16[1024,224]{0,1:T(8,128)(2,1)}, u32[]{:S(2)}, u32[]{:S(2)}) collective-permute-start(bf16[1024,224]{0,1:T(8,128)(2,1)S(1)} %collective-permute-done.3), channel_id=1, source_target_pairs={{0,120},{8,0},{16,8},{24,16},{32,24},{40,32},{48,40},{56,48},{64,5... | collective-permute-start | bytes 1376264 | tf_op jit(solution)/shard_map/ppermute | solution.py:20
  50.6 12.2 %copy-start.10 = (bf16[1024,224]{0,1:T(8,128)(2,1)}, bf16[1024,224]{0,1:T(8,128)(2,1)S(1)}, u32[]{:S(2)}) copy-start(bf16[1024,224]{0,1:T(8,128)(2,1)S(1)} %collective-permute-done.4) | copy-start | bytes 1376260
  50.6 12.2 %collective-permute-start.6 = (bf16[1024,224]{0,1:T(8,128)(2,1)S(1)}, bf16[1024,224]{0,1:T(8,128)(2,1)S(1)}, u32[]{:S(2)}, u32[]{:S(2)}) collective-permute-start(bf16[1024,224]{0,1:T(8,128)(2,1)S(1)} %collective-permute-done.4), channel_id=1, source_target_pairs={{0,8},{8,16},{16,24},{24,32},{32,40},{40,48},{48,56},{56,64},{64,7... | collective-permute-start | bytes 1376264 | tf_op jit(solution)/shard_map/ppermute | solution.py:17
  50.7 13.6 %collective-permute-start.7 = (bf16[1024,224]{0,1:T(8,128)(2,1)}, bf16[1024,224]{0,1:T(8,128)(2,1)}, u32[]{:S(2)}, u32[]{:S(2)}) collective-permute-start(bf16[1024,224]{0,1:T(8,128)(2,1)} %collective-permute-done.5), channel_id=1, source_target_pairs={{0,120},{8,0},{16,8},{24,16},{32,24},{40,32},{48,40},{56,48},{64,5... | collective-permute-start | bytes 1376264 | tf_op jit(solution)/shard_map/ppermute | solution.py:20
  62.9 11.4 %collective-permute-start.8 = (bf16[1024,224]{0,1:T(8,128)(2,1)S(1)}, bf16[1024,224]{0,1:T(8,128)(2,1)}, u32[]{:S(2)}, u32[]{:S(2)}) collective-permute-start(bf16[1024,224]{0,1:T(8,128)(2,1)S(1)} %collective-permute-done.6), channel_id=1, source_target_pairs={{0,8},{8,16},{16,24},{24,32},{32,40},{40,48},{48,56},{56,64},{64,7... | collective-permute-start | bytes 1376264 | tf_op jit(solution)/shard_map/ppermute | solution.py:17
  63.2 11.1 %copy-start.7 = (bf16[1024,224]{0,1:T(8,128)(2,1)S(1)}, bf16[1024,224]{0,1:T(8,128)(2,1)}, u32[]{:S(2)}) copy-start(bf16[1024,224]{0,1:T(8,128)(2,1)} %copy-done.6) | copy-start | bytes 1376260
  63.2 11.1 %copy-start.11 = (bf16[1024,224]{0,1:T(8,128)(2,1)S(1)}, bf16[1024,224]{0,1:T(8,128)(2,1)}, u32[]{:S(2)}) copy-start(bf16[1024,224]{0,1:T(8,128)(2,1)} %copy-done.10) | copy-start | bytes 1376260
  64.3 10.3 %collective-permute-start.9 = (bf16[1024,224]{0,1:T(8,128)(2,1)}, bf16[1024,224]{0,1:T(8,128)(2,1)S(1)}, u32[]{:S(2)}, u32[]{:S(2)}) collective-permute-start(bf16[1024,224]{0,1:T(8,128)(2,1)} %collective-permute-done.7), channel_id=1, source_target_pairs={{0,120},{8,0},{16,8},{24,16},{32,24},{40,32},{48,40},{56,48},{64,5... | collective-permute-start | bytes 1376264 | tf_op jit(solution)/shard_map/ppermute | solution.py:20
  74.2 10.9 %collective-permute-start.10 = (bf16[1024,224]{0,1:T(8,128)(2,1)}, bf16[1024,224]{0,1:T(8,128)(2,1)S(1)}, u32[]{:S(2)}, u32[]{:S(2)}) collective-permute-start(bf16[1024,224]{0,1:T(8,128)(2,1)} %collective-permute-done.8), channel_id=1, source_target_pairs={{0,8},{8,16},{16,24},{24,32},{32,40},{40,48},{48,56},{56,64},{64,7... | collective-permute-start | bytes 1376264 | tf_op jit(solution)/shard_map/ppermute | solution.py:17
  74.5 12.7 %collective-permute-start.11 = (bf16[1024,224]{0,1:T(8,128)(2,1)S(1)}, bf16[1024,224]{0,1:T(8,128)(2,1)S(1)}, u32[]{:S(2)}, u32[]{:S(2)}) collective-permute-start(bf16[1024,224]{0,1:T(8,128)(2,1)S(1)} %collective-permute-done.9), channel_id=1, source_target_pairs={{0,120},{8,0},{16,8},{24,16},{32,24},{40,32},{48,40},{56,48},{64,5... | collective-permute-start | bytes 1376264 | tf_op jit(solution)/shard_map/ppermute | solution.py:20
  85.1 10.6 %collective-permute-start.12 = (bf16[1024,224]{0,1:T(8,128)(2,1)S(1)}, bf16[1024,224]{0,1:T(8,128)(2,1)S(1)}, u32[]{:S(2)}, u32[]{:S(2)}) collective-permute-start(bf16[1024,224]{0,1:T(8,128)(2,1)S(1)} %collective-permute-done.10), channel_id=1, source_target_pairs={{0,8},{8,16},{16,24},{24,32},{32,40},{40,48},{48,56},{56,64},{64,7... | collective-permute-start | bytes 1376264 | tf_op jit(solution)/shard_map/ppermute | solution.py:17
  87.3 10.3 %collective-permute-start.13 = (bf16[1024,224]{0,1:T(8,128)(2,1)S(1)}, bf16[1024,224]{0,1:T(8,128)(2,1)S(1)}, u32[]{:S(2)}, u32[]{:S(2)}) collective-permute-start(bf16[1024,224]{0,1:T(8,128)(2,1)S(1)} %collective-permute-done.11), channel_id=1, source_target_pairs={{0,120},{8,0},{16,8},{24,16},{32,24},{40,32},{48,40},{56,48},{64,5... | collective-permute-start | bytes 1376264 | tf_op jit(solution)/shard_map/ppermute | solution.py:20
  95.8 11.5 %collective-permute-start.14 = (bf16[1024,224]{0,1:T(8,128)(2,1)S(1)}, bf16[1024,224]{0,1:T(8,128)(2,1)S(1)}, u32[]{:S(2)}, u32[]{:S(2)}) collective-permute-start(bf16[1024,224]{0,1:T(8,128)(2,1)S(1)} %collective-permute-done.12), channel_id=1, source_target_pairs={{0,8},{8,16},{16,24},{24,32},{32,40},{40,48},{48,56},{56,64},{64,7... | collective-permute-start | bytes 1376264 | tf_op jit(solution)/shard_map/ppermute | solution.py:17
  127.1 51.8 %copy-start.3 = (bf16[128,3584]{1,0:T(8,128)(2,1)S(1)}, bf16[128,3584]{1,0:T(8,128)(2,1)}, u32[]{:S(2)}) copy-start(bf16[128,3584]{1,0:T(8,128)(2,1)} %param.13) | copy-start | bytes 2752516
  127.1 53.4 %copy-start.14 = (f32[3584]{0:T(1024)S(1)}, f32[3584]{0:T(1024)}, u32[]{:S(2)}) copy-start(f32[3584]{0:T(1024)} %param.14) | copy-start | bytes 43012
  204.7 200.6 %all-to-all-start = ((bf16[128,12,3584]{2,1,0:T(8,128)(2,1)}), bf16[128,12,3584]{2,1,0:T(8,128)(2,1)}, u32[]{:S(2)}, u32[]{:S(2)}) async-start(bf16[128,12,3584]{2,1,0:T(8,128)(2,1)} %reshape.85), calls=%async_computation | async-start | bytes 29360128 | tf_op jit(solution)/shard_map/all_to_all | solution.py:79
  422.4 16.6 %copy-start.2 = (bf16[1536,3584]{1,0:T(8,128)(2,1)S(1)}, bf16[1536,3584]{1,0:T(8,128)(2,1)}, u32[]{:S(2)}) copy-start(bf16[1536,3584]{1,0:T(8,128)(2,1)} %reshape.86) | copy-start | bytes 33030148
  422.4 34.9 %slice-start = ((s8[7340032]{0:T(1024)(128)(4,1)}), s8[4194304]{0:T(1024)(128)(4,1)S(1)}, s32[]{:S(2)}) async-start(s8[7340032]{0:T(1024)(128)(4,1)} %bitcast.43), calls=%async_computation.4 | async-start | bytes 8388608
  439.0 18.3 %slice-start.1 = ((s8[7340032]{0:T(1024)(128)(4,1)}), s8[3145728]{0:T(1024)(128)(4,1)S(1)}, s32[]{:S(2)}) async-start(s8[7340032]{0:T(1024)(128)(4,1)} %bitcast.43), calls=%async_computation.5 | async-start | bytes 6291456
  491.6 14.5 %copy-start.16 = (f32[128,8]{0,1:T(8,128)S(1)}, f32[128,8]{0,1:T(8,128)}, u32[]{:S(2)}) copy-start(f32[128,8]{0,1:T(8,128)} %param.16) | copy-start | bytes 12292
  491.6 205.8 %all-to-all-start.1 = ((bf16[128,12,3584]{2,1,0:T(8,128)(2,1)}), bf16[128,12,3584]{2,1,0:T(8,128)(2,1)}, u32[]{:S(2)}, u32[]{:S(2)}) async-start(bf16[128,12,3584]{2,1,0:T(8,128)(2,1)} %reshape.87), calls=%async_computation.1 | async-start | bytes 29360128 | tf_op jit(solution)/shard_map/all_to_all | solution.py:94
  714.5 102.7 %copy-start.1 = (bf16[1024,1024]{1,0:T(8,128)(2,1)S(1)}, bf16[1024,1024]{1,0:T(8,128)(2,1)}, u32[]{:S(2)}) copy-start(bf16[1024,1024]{1,0:T(8,128)(2,1)} %param.11) | copy-start | bytes 6291460
  (7 other events, 33.8 us)
Sparse Core Ops, SparseCore 0:
  127.3 51.6 reduce-scatter.3
